TPU v7x, 32 devices: a whole 2x2x4 slice. The times are simulated.
32 devices in a mesh: groups: 2 (over y), hid: 4 (over z), rows: 2 (over x), mp: 2 (over core).
Axes of the slice: x: 2, y: 2, z: 4, core: 2. Of those that a mesh axis runs over, the one named last changes fastest.
Arguments:
- tokens: bfloat16 [1024, 4096], P(('groups', 'rows'), 'hid'), parts along dimension 0, may hold values from -6 to 6
- norm_gain: float32 [2, 4096], P('mp'), may hold values from 0.1 to 1.9
- gate_weight: bfloat16 [2, 4096, 14336], P('mp', 'rows', 'hid'), may hold values from -0.09375 to 0.09375
- up_weight: bfloat16 [2, 4096, 14336], P('mp', 'rows', 'hid'), may hold values from -0.09375 to 0.09375
- down_weight: bfloat16 [2, 14336, 4096], P('mp', 'hid', 'rows'), may hold values from -0.046875 to 0.046875
- enc_weight: bfloat16 [2, 4096, 16384], P('mp', 'rows', 'hid'), may hold values from -0.0625 to 0.0625
- enc_bias: float32 [16384], P('hid'), may hold values from -3 to 3
- adjoint: bfloat16 [1024, 16384], P(('groups', 'rows', 'mp'), 'hid'), parts along dimension 0, may hold values from -6 to 6
Outputs:
- gated: bfloat16 [1024, 16384], P(('groups', 'rows', 'mp'), 'hid'), parts along dimension 0
There are 2 independent parts, one for each index of `groups`. A program takes and returns all parts, laid end to end along the dimension named above; an argument that names none is the same for every part. Nothing has to cross between parts.
All inputs are finite; a program needn't handle non-finite values.
Results may differ from a plain program's by a relative error of at most 0.0058.
Values may be sent and summed in bfloat16 or wider, within the bound.
A program may use at most 128 MiB of HBM per device.

v0:
```python
import jax
import jax.numpy as jnp
from jax import lax
from jax.sharding import PartitionSpec as P


def on_device(
    tokens, norm_gain, gate_weight, up_weight, down_weight, enc_weight, enc_bias, adjoint
):
    gathered = lax.all_gather(tokens, "hid", axis=1, tiled=True)
    tokens_float = gathered.astype(jnp.float32)
    inverse_rms = lax.rsqrt(jnp.mean(tokens_float * tokens_float, axis=-1, keepdims=True) + 1e-05)
    normed = (tokens_float * inverse_rms * norm_gain[0][None, :]).astype(jnp.bfloat16)
    gate_local = gate_weight[0]
    up_local = up_weight[0]
    hidden_width = gate_local.shape[1]
    all_normed = lax.all_gather(normed, "rows", axis=0, tiled=True)
    width_rows = gate_local.shape[0]
    column_start = lax.axis_index("rows") * width_rows
    own_columns = lax.dynamic_slice_in_dim(all_normed, column_start, width_rows, 1)
    both_local = jnp.concatenate((gate_local, up_local), axis=1)
    selected = own_columns
    summed = lax.psum_scatter(
        jnp.dot(selected, both_local, preferred_element_type=jnp.float32),
        "rows",
        scatter_dimension=0,
        tiled=True,
    )
    gate_acts = summed[:, :hidden_width]
    up_acts = summed[:, hidden_width:]
    hidden = (jax.nn.silu(gate_acts) * up_acts).astype(jnp.bfloat16)
    down_local = down_weight[0]
    partial_out = jnp.dot(
        lax.all_gather(hidden, "rows", axis=0, tiled=True),
        down_local,
        preferred_element_type=jnp.float32,
    )
    block_out = lax.psum(partial_out, "hid").astype(jnp.bfloat16)
    enc_local = enc_weight[0]
    selected = block_out
    pre_rows = lax.psum_scatter(
        jnp.dot(selected, enc_local, preferred_element_type=jnp.float32),
        ("rows", "mp"),
        scatter_dimension=0,
        tiled=True,
    )
    pre_rows = pre_rows + enc_bias[None, :]
    return (jnp.maximum(pre_rows, 0.0) * adjoint.astype(jnp.float32)).astype(jnp.bfloat16)


def solution(mesh):
    placed = (
        P(("groups", "rows"), "hid"),
        P("mp", None),
        P("mp", "rows", "hid"),
        P("mp", "rows", "hid"),
        P("mp", "hid", "rows"),
        P("mp", "rows", "hid"),
        P("hid"),
        P(("groups", "rows", "mp"), "hid"),
    )
    return jax.shard_map(
        on_device,
        mesh=mesh,
        in_specs=placed,
        out_specs=P(("groups", "rows", "mp"), "hid"),
        check_vma=False,
    )
```

profile of v0, /device:TPU:0, one launch (start us, length us, event | category | flops | bytes accessed | tf_op | source)
XLA Modules:
  0.0 619.3 jit_solution(2788526948449439029)
XLA Ops:
  6.5 0.0 all-gather.4.cloned.1.call-start
  6.5 0.7 all-gather.4.cloned.1.call-update
  7.3 0.0 all-gather.6.cloned.1.call-start
  7.3 50.0 %all-gather.4.cloned.1.call-done = bf16[256,4096]{1,0:T(8,128)(2,1)} async-done(((bf16[256,1024]{1,0:T(8,128)(2,1)}), bf16[256,4096]{1,0:T(8,128)(2,1)}) %all-gather.4.cloned.1.call-update) | async-done | bytes 2097168 | tf_op jit(solution)/shard_map/all_gather | solution.py:10
  57.3 2.1 fusion.8
  59.4 3.6 fusion.10
  63.0 0.0 all-gather.6.cloned.1.call-update
  63.0 0.0 reduce-scatter.3.cloned.1.call-start
  63.1 55.6 %all-gather.6.cloned.1.call-done = bf16[512,4096]{1,0:T(8,128)(2,1)} async-done(((bf16[256,4096]{1,0:T(8,128)(2,1)}), bf16[512,4096]{1,0:T(8,128)(2,1)}) %all-gather.6.cloned.1.call-update) | async-done | bytes 4194320 | tf_op jit(solution)/shard_map/all_gather | solution.py:17
  118.7 22.1 %fusion = f32[512,7168]{1,0:T(8,128)} fusion(bf16[2048,3584]{1,0:T(8,128)(2,1)} %bitcast.12, bf16[2048,3584]{1,0:T(8,128)(2,1)} %bitcast.13, bf16[512,4096]{1,0:T(8,128)(2,1)} %all-gather.6.cloned.1.call-done, s32[]{:T(128)S(6)} %select_n.3), kind=kOutput, calls=%fused_computation | convolution fusion | flops 15091105792 | bytes 46137348 | tf_op jit(solution)/shard_map/dot_general | solution.py:24
  140.8 0.0 reduce-scatter.3.cloned.1.call-update
  140.8 0.0 all-gather.8.cloned.1.call-start
  140.9 167.3 %reduce-scatter.3.cloned.1.call-done = f32[256,7168]{1,0:T(8,128)} async-done(((f32[512,7168]{1,0:T(8,128)}), f32[256,7168]{1,0:T(8,128)}) %reduce-scatter.3.cloned.1.call-update) | async-done | bytes 7340048 | tf_op jit(solution)/shard_map/reduce_scatter | solution.py:23
  308.1 5.5 fusion.11
  313.6 0.0 all-gather.8.cloned.1.call-update
  313.6 0.0 reduce-scatter.5.cloned.1.call-start
  313.7 50.9 %all-gather.8.cloned.1.call-done = bf16[512,3584]{1,0:T(8,128)(2,1)} async-done(((bf16[256,3584]{1,0:T(8,128)(2,1)}), bf16[512,3584]{1,0:T(8,128)(2,1)}) %all-gather.8.cloned.1.call-update) | async-done | bytes 3670032 | tf_op jit(solution)/shard_map/all_gather | solution.py:34
  364.6 13.4 %fusion.6 = f32[512,2048]{1,0:T(8,128)} fusion(bf16[512,3584]{1,0:T(8,128)(2,1)} %all-gather.8.cloned.1.call-done, bf16[1,3584,2048]{2,1,0:T(8,128)(2,1)} %param.12), kind=kOutput, calls=%fused_computation.6 | convolution fusion | flops 7516192768 | bytes 22544384 | tf_op jit(solution)/shard_map/dot_general | solution.py:33
  378.0 148.0 %all-reduce.1 = bf16[512,2048]{1,0:T(8,128)(2,1)S(1)} all-reduce(f32[512,2048]{1,0:T(8,128)} %fusion.6), channel_id=1, replica_groups=mesh['groups'=2,'hid'=4,'rows'=2,'mp'=2] {'hid'}, use_global_device_ids=true, to_apply=%region_2.3 | all-reduce | flops 1048576 | bytes 6291456 | tf_op jit(solution)/shard_map/psum | solution.py:38
  526.0 14.4 %fusion.4 = f32[512,4096]{1,0:T(8,128)} fusion(bf16[1,2048,4096]{2,1,0:T(8,128)(2,1)} %param.13, bf16[512,2048]{1,0:T(8,128)(2,1)S(1)} %all-reduce.1), kind=kOutput, calls=%fused_computation.4 | convolution fusion | flops 8589934592 | bytes 27262976 | tf_op jit(solution)/shard_map/dot_general | solution.py:42
  540.4 0.0 copy-start
  540.4 0.0 copy-start.1
  540.4 0.0 reduce-scatter.5.cloned.1.call-update
  540.4 69.5 %reduce-scatter.5.cloned.1.call-done = f32[128,4096]{1,0:T(8,128)} async-done(((f32[512,4096]{1,0:T(8,128)}), f32[128,4096]{1,0:T(8,128)}) %reduce-scatter.5.cloned.1.call-update) | async-done | bytes 2097168 | tf_op jit(solution)/shard_map/reduce_scatter | solution.py:41
  609.9 0.0 copy-done
  609.9 0.0 copy-done.1
  609.9 2.9 multiply_convert_fusion
  (1 shorter events, 0.0 us)
Async XLA Ops:
  6.5 50.8 %all-gather.4.cloned.1.call-start = ((), (), s32[]{:S(2)}) async-start(), calls=%async_computation.2 | async-start | bytes 2621440 | tf_op jit(solution)/shard_map/all_gather | solution.py:10
  7.3 111.4 %all-gather.6.cloned.1.call-start = ((), (), s32[]{:S(2)}) async-start(), calls=%async_computation.3 | async-start | bytes 6291456 | tf_op jit(solution)/shard_map/all_gather | solution.py:17
  63.0 245.1 %reduce-scatter.3.cloned.1.call-start = ((), (), s32[]{:S(2)}) async-start(), calls=%async_computation.4 | async-start | bytes 22020096 | tf_op jit(solution)/shard_map/reduce_scatter | solution.py:23
  140.8 223.8 %all-gather.8.cloned.1.call-start = ((), (), s32[]{:S(2)}) async-start(), calls=%async_computation.5 | async-start | bytes 5505024 | tf_op jit(solution)/shard_map/all_gather | solution.py:34
  313.6 296.3 %reduce-scatter.5.cloned.1.call-start = ((), (), s32[]{:S(2)}) async-start(), calls=%async_computation.6 | async-start | bytes 10485760 | tf_op jit(solution)/shard_map/reduce_scatter | solution.py:41
  540.4 69.5 %copy-start = (bf16[128,4096]{1,0:T(8,128)(2,1)S(1)}, bf16[128,4096]{1,0:T(8,128)(2,1)}, u32[]{:S(2)}) copy-start(bf16[128,4096]{1,0:T(8,128)(2,1)} %param.15) | copy-start | bytes 3145732
  540.4 69.5 %copy-start.1 = (f32[4096]{0:T(1024)S(1)}, f32[4096]{0:T(1024)}, u32[]{:S(2)}) copy-start(f32[4096]{0:T(1024)} %param.14) | copy-start | bytes 49156
Sparse Core Ops, SparseCore 0:
  8.9 48.3 all-gather.3
  63.1 55.5 all-gather.5
  141.0 167.1 reduce-scatter.2
  313.7 50.8 all-gather.7
  540.5 69.3 reduce-scatter.4
where the time goes:
time: 620 us; the launch traced here: 619 us
  waiting for transfers between devices  394 us (64%)
  blocking collectives  148 us (24%)
  matrix products  49.9 us (8%)
  other arithmetic  14 us (2%)
  between operations  13.2 us (2%)
    reduce_scatter x1, waiting for transfers between devices, on_device(): lax.psum_scatter(jnp.dot(selected, both_local, preferred_element_type=jnp...  167 us
    psum x1, blocking collectives, on_device(): block_out = lax.psum(partial_out, 'hid').astype(jnp.bfloat16)  148 us
    reduce_scatter x1, waiting for transfers between devices, on_device(): lax.psum_scatter(jnp.dot(selected, enc_local, preferred_element_type=jnp....  69.5 us
    all_gather x1, waiting for transfers between devices, on_device(): all_normed = lax.all_gather(normed, 'rows', axis=0, tiled=True)  55.6 us
    all_gather x1, waiting for transfers between devices, on_device(): lax.all_gather(hidden, 'rows', axis=0, tiled=True)  50.9 us
    all_gather x1, waiting for transfers between devices, on_device(): gathered = lax.all_gather(tokens, 'hid', axis=1, tiled=True)  50 us
    dot_general x1, matrix products, on_device(): jnp.dot(selected, both_local, preferred_element_type=jnp.float32)  22.1 us
    dot_general x1, matrix products, on_device(): jnp.dot(selected, enc_local, preferred_element_type=jnp.float32)  14.4 us
  transfers between devices with their start and end apart: 5, of which 5 were waited for; matrix products, arithmetic and copies ran while one was open for 0% of the time, Pallas kernels for 0%

commit v1 on v0

--- a/solution.py
+++ b/solution.py
@@ -35,7 +35,8 @@
         down_local,
         preferred_element_type=jnp.float32,
     )
-    block_out = lax.psum(partial_out, "hid").astype(jnp.bfloat16)
+    order_shapes_here = lambda arr_in: jnp.sum(jax.lax.all_gather(arr_in, "hid"), axis=0)
+    block_out = order_shapes_here(partial_out).astype(jnp.bfloat16)
     enc_local = enc_weight[0]
     selected = block_out
     pre_rows = lax.psum_scatter(

time: 620 us -> 767 us (1.24)
  waiting for transfers between devices: 394 us -> 681 us
  blocking collectives: 148 us -> 0 us
  other arithmetic: 14 us -> 22.1 us
    all_gather x0 -> x1, waiting for transfers between devices: none -> 287 us  [on_device(): jax.lax.all_gather(arr_in, 'hid')]
    psum x1 -> x0, blocking collectives: 148 us -> none  [on_device(): block_out = lax.psum(partial_out, 'hid').astype(jnp.bfloat16)]
    reduce_sum x0 -> x1, other arithmetic: none -> 8.11 us  [on_device(): jnp.sum(jax.lax.all_gather(arr_in, 'hid'), axis=0)]
  transfers between devices with their start and end apart: 5 -> 6, of which waited for: 5 -> 6; matrix products, arithmetic and copies ran while one was open for 0% -> 0% of each run, Pallas kernels for 0% -> 0%
where the time goes in v1:
time: 767 us
  waiting for transfers between devices  681 us (89%)
  matrix products  50 us (7%)
  other arithmetic  22.1 us (3%)
  between operations  13.5 us (2%)
    all_gather x1, waiting for transfers between devices, on_device(): jax.lax.all_gather(arr_in, 'hid')  287 us
    reduce_scatter x1, waiting for transfers between devices, on_device(): lax.psum_scatter(jnp.dot(selected, both_local, preferred_element_type=jnp...  167 us
    reduce_scatter x1, waiting for transfers between devices, on_device(): lax.psum_scatter(jnp.dot(selected, enc_local, preferred_element_type=jnp....  69.7 us
    all_gather x1, waiting for transfers between devices, on_device(): all_normed = lax.all_gather(normed, 'rows', axis=0, tiled=True)  55.6 us
    all_gather x1, waiting for transfers between devices, on_device(): lax.all_gather(hidden, 'rows', axis=0, tiled=True)  50.9 us
    all_gather x1, waiting for transfers between devices, on_device(): gathered = lax.all_gather(tokens, 'hid', axis=1, tiled=True)  50 us
    dot_general x1, matrix products, on_device(): jnp.dot(selected, both_local, preferred_element_type=jnp.float32)  22.2 us
  transfers between devices with their start and end apart: 6, of which 6 were waited for; matrix products, arithmetic and copies ran while one was open for 0% of the time, Pallas kernels for 0%

profile of v1, /device:TPU:0, one launch (start us, length us, event | category | flops | bytes accessed | tf_op | source)
XLA Modules:
  0.0 767.1 jit_solution(15519418914967437444)
XLA Ops:
  6.5 0.0 all-gather.6.cloned.1.call-start
  6.5 0.7 all-gather.6.cloned.1.call-update
  7.3 0.0 all-gather.8.cloned.1.call-start
  7.3 50.0 %all-gather.6.cloned.1.call-done = bf16[256,4096]{1,0:T(8,128)(2,1)} async-done(((bf16[256,1024]{1,0:T(8,128)(2,1)}), bf16[256,4096]{1,0:T(8,128)(2,1)}) %all-gather.6.cloned.1.call-update) | async-done | bytes 2097168 | tf_op jit(solution)/shard_map/all_gather | solution.py:10
  57.3 2.1 fusion.8
  59.4 3.6 fusion.10
  63.0 0.0 all-gather.8.cloned.1.call-update
  63.0 0.0 reduce-scatter.3.cloned.1.call-start
  63.1 55.6 %all-gather.8.cloned.1.call-done = bf16[512,4096]{1,0:T(8,128)(2,1)} async-done(((bf16[256,4096]{1,0:T(8,128)(2,1)}), bf16[512,4096]{1,0:T(8,128)(2,1)}) %all-gather.8.cloned.1.call-update) | async-done | bytes 4194320 | tf_op jit(solution)/shard_map/all_gather | solution.py:17
  118.7 22.2 %fusion = f32[512,7168]{1,0:T(8,128)} fusion(bf16[2048,3584]{1,0:T(8,128)(2,1)} %bitcast.14, bf16[2048,3584]{1,0:T(8,128)(2,1)} %bitcast.15, bf16[512,4096]{1,0:T(8,128)(2,1)} %all-gather.8.cloned.1.call-done, s32[]{:T(128)S(6)} %select_n.3), kind=kOutput, calls=%fused_computation | convolution fusion | flops 15091105792 | bytes 46137348 | tf_op jit(solution)/shard_map/dot_general | solution.py:24
  140.9 0.0 reduce-scatter.3.cloned.1.call-update
  140.9 0.0 all-gather.10.cloned.1.call-start
  141.0 167.3 %reduce-scatter.3.cloned.1.call-done = f32[256,7168]{1,0:T(8,128)} async-done(((f32[512,7168]{1,0:T(8,128)}), f32[256,7168]{1,0:T(8,128)}) %reduce-scatter.3.cloned.1.call-update) | async-done | bytes 7340048 | tf_op jit(solution)/shard_map/reduce_scatter | solution.py:23
  308.2 5.5 fusion.11
  313.7 0.0 all-gather.10.cloned.1.call-update
  313.7 0.0 all-gather.12.cloned.1.call-start
  313.8 50.9 %all-gather.10.cloned.1.call-done = bf16[512,3584]{1,0:T(8,128)(2,1)} async-done(((bf16[256,3584]{1,0:T(8,128)(2,1)}), bf16[512,3584]{1,0:T(8,128)(2,1)}) %all-gather.10.cloned.1.call-update) | async-done | bytes 3670032 | tf_op jit(solution)/shard_map/all_gather | solution.py:34
  364.7 13.5 %fusion.6 = f32[512,2048]{1,0:T(8,128)} fusion(bf16[512,3584]{1,0:T(8,128)(2,1)} %all-gather.10.cloned.1.call-done, bf16[1,3584,2048]{2,1,0:T(8,128)(2,1)} %param.12), kind=kOutput, calls=%fused_computation.6 | convolution fusion | flops 7516192768 | bytes 22544384 | tf_op jit(solution)/shard_map/dot_general | solution.py:33
  378.2 0.0 all-gather.12.cloned.1.call-update
  378.2 0.2 reduce-scatter.5.cloned.1.call-start
  378.4 286.7 %all-gather.12.cloned.1.call-done = f32[2048,2048]{1,0:T(8,128)} async-done(((f32[512,2048]{1,0:T(8,128)}), f32[2048,2048]{1,0:T(8,128)}) %all-gather.12.cloned.1.call-update) | async-done | bytes 16777232 | tf_op jit(solution)/shard_map/all_gather | solution.py:38
  665.1 8.1 %reduce_sum.19 = bf16[512,2048]{1,0:T(8,128)(2,1)S(1)} reduce(f32[4,512,2048]{2,1,0:T(8,128)} %bitcast.12, f32[]{:T(128)} %constant.8.clone.1), dimensions={0}, to_apply=%region_2.3 | reduce | flops 3145728 | bytes 18874372 | tf_op jit(solution)/shard_map/reduce_sum | solution.py:38
  673.2 14.4 %fusion.4 = f32[512,4096]{1,0:T(8,128)} fusion(bf16[1,2048,4096]{2,1,0:T(8,128)(2,1)} %param.13, bf16[512,2048]{1,0:T(8,128)(2,1)S(1)} %reduce_sum.19), kind=kOutput, calls=%fused_computation.4 | convolution fusion | flops 8589934592 | bytes 27262976 | tf_op jit(solution)/shard_map/dot_general | solution.py:43
  687.6 0.0 copy-start
  687.6 0.0 copy-start.1
  687.6 0.0 reduce-scatter.5.cloned.1.call-update
  687.6 69.7 %reduce-scatter.5.cloned.1.call-done = f32[128,4096]{1,0:T(8,128)} async-done(((f32[512,4096]{1,0:T(8,128)}), f32[128,4096]{1,0:T(8,128)}) %reduce-scatter.5.cloned.1.call-update) | async-done | bytes 2097168 | tf_op jit(solution)/shard_map/reduce_scatter | solution.py:42
  757.4 0.0 copy-done
  757.4 0.0 copy-done.1
  757.4 2.9 multiply_convert_fusion
  (1 shorter events, 0.0 us)
Async XLA Ops:
  6.5 50.8 %all-gather.6.cloned.1.call-start = ((), (), s32[]{:S(2)}) async-start(), calls=%async_computation.2 | async-start | bytes 2621440 | tf_op jit(solution)/shard_map/all_gather | solution.py:10
  7.3 111.4 %all-gather.8.cloned.1.call-start = ((), (), s32[]{:S(2)}) async-start(), calls=%async_computation.3 | async-start | bytes 6291456 | tf_op jit(solution)/shard_map/all_gather | solution.py:17
  63.0 245.2 %reduce-scatter.3.cloned.1.call-start = ((), (), s32[]{:S(2)}) async-start(), calls=%async_computation.4 | async-start | bytes 22020096 | tf_op jit(solution)/shard_map/reduce_scatter | solution.py:23
  140.9 223.8 %all-gather.10.cloned.1.call-start = ((), (), s32[]{:S(2)}) async-start(), calls=%async_computation.5 | async-start | bytes 5505024 | tf_op jit(solution)/shard_map/all_gather | solution.py:34
  313.7 351.4 %all-gather.12.cloned.1.call-start = ((), (), s32[]{:S(2)}) async-start(), calls=%async_computation.7 | async-start | bytes 20971520 | tf_op jit(solution)/shard_map/all_gather | solution.py:38
  378.2 379.2 %reduce-scatter.5.cloned.1.call-start = ((), (), s32[]{:S(2)}) async-start(), calls=%async_computation.6 | async-start | bytes 10485760 | tf_op jit(solution)/shard_map/reduce_scatter | solution.py:42
  687.6 69.8 %copy-start = (bf16[128,4096]{1,0:T(8,128)(2,1)S(1)}, bf16[128,4096]{1,0:T(8,128)(2,1)}, u32[]{:S(2)}) copy-start(bf16[128,4096]{1,0:T(8,128)(2,1)} %param.15) | copy-start | bytes 3145732
  687.6 69.8 %copy-start.1 = (f32[4096]{0:T(1024)S(1)}, f32[4096]{0:T(1024)}, u32[]{:S(2)}) copy-start(f32[4096]{0:T(1024)} %param.14) | copy-start | bytes 49156
Sparse Core Ops, SparseCore 0:
  8.9 48.3 all-gather.5
  63.1 55.5 all-gather.7
  141.0 167.1 reduce-scatter.2
  313.9 50.8 all-gather.9
  378.3 286.7 all-gather.11
  687.7 69.5 reduce-scatter.4
